TPU v7x, 256 devices: a whole 4x4x8 slice. The times are simulated.
256 devices in a mesh: rows: 64 (over z, y, x_hi), panel: 4 (over x_lo, core).
Axes of the slice: x: 4 (x_hi: 2, x_lo: 2; x = x_hi * 2 + x_lo), y: 4, z: 8, core: 2. Of those that a mesh axis runs over, the one named last changes fastest.
Arguments:
- acts: bfloat16 [262144, 4096], P('rows', 'panel'), may hold values from -16 to 16
- basis: bfloat16 [4096, 256], P('panel'), may hold values from -0.09375 to 0.09375
- center: float32 [4096], P('panel'), may hold values from -6 to 6
- mask: int32 [262144], P('rows'), may hold values 0 or 1
Outputs:
- orthonormal: float32 [4096, 256], P('panel')
- scores: bfloat16 [262144, 256], P(('rows', 'panel'))
- subset_mean: float32 [256], replicated
- subset_cov: float32 [256, 256], replicated
Inputs may be any that keep to these rules, and one draw needn't show every extreme that they name: `mask`: 1 marks a row of the h-subset.
All inputs are finite; a program needn't handle non-finite values. No bound on the sum of `mask` on one device may be relied on, other than what follows from the above.
Results may differ from a plain program's by a relative error of at most 0.0042.
Values may be sent and summed in bfloat16 or wider, within the bound.
A program may use at most 64 MiB of HBM per device.

v0:
```python
import jax
import jax.numpy as jnp
from jax import lax
from jax.sharding import PartitionSpec as P


def moments_of(score_half, mask_part):
    weight_sum = jnp.sum(mask_part.astype(jnp.float32))
    mask_half = mask_part.astype(jnp.bfloat16)
    first_moment = jnp.dot(mask_half, score_half, preferred_element_type=jnp.float32)
    second_moment = lax.dot_general(
        score_half * mask_half[:, None],
        score_half,
        (((0,), (0,)), ((), ())),
        preferred_element_type=jnp.float32,
    )
    return (weight_sum, first_moment, second_moment)


def per_device(acts, basis, center, mask):
    high = lax.Precision.HIGHEST
    row_count = acts.shape[0]
    rows_total = row_count * lax.axis_size("rows")
    panels = lax.axis_size("panel")
    partial_proj = jnp.dot(acts, basis, preferred_element_type=jnp.float32)
    projected = lax.psum(partial_proj, "panel").astype(jnp.bfloat16)
    cross_term = lax.dot_general(
        acts, projected, (((0,), (0,)), ((), ())), preferred_element_type=jnp.float32
    )
    crossed = lax.psum(cross_term, "rows") / jnp.float32(rows_total) + basis.astype(jnp.float32)
    gram_matrix = lax.psum(jnp.dot(crossed.T, crossed, precision=high), "panel")
    factor = jnp.linalg.cholesky(gram_matrix)
    orthonormal = lax.linalg.triangular_solve(
        factor, crossed, left_side=False, lower=True, transpose_a=True
    )
    offset_part = jnp.dot(center, orthonormal, precision=high)
    ortho_half = orthonormal.astype(jnp.bfloat16)
    quarter = row_count // panels
    score_part = (
        jnp.dot(acts, ortho_half, preferred_element_type=jnp.float32) - offset_part[None, :]
    )
    score_half = lax.psum(score_part, "panel").astype(jnp.bfloat16)
    totals = lax.psum(moments_of(score_half, mask), "rows")
    scores = lax.dynamic_slice_in_dim(score_half, lax.axis_index("panel") * quarter, quarter, 0)
    weight_sum, first_moment, second_moment = totals
    subset_mean = first_moment / jnp.maximum(weight_sum, 1.0)
    subset_cov = (second_moment - weight_sum * jnp.outer(subset_mean, subset_mean)) / jnp.maximum(
        weight_sum - 1.0, 1.0
    )
    return (orthonormal, scores, subset_mean, subset_cov)


def solution(mesh):
    placed = (P("rows", "panel"), P("panel", None), P("panel"), P("rows"))
    return jax.shard_map(
        per_device,
        mesh=mesh,
        in_specs=placed,
        out_specs=(P("panel", None), P(("rows", "panel"), None), P(), P()),
        check_vma=False,
    )
```

profile of v0, /device:TPU:1, one launch (start us, length us, event | category | flops | bytes accessed | tf_op | source)
XLA Modules:
  0.0 1628.0 jit_solution(4723854596054861623)
XLA Ops:
  7.2 0.0 copy-start
  7.2 0.0 all-reduce.8.cloned.1.call-start
  7.2 7.7 fusion.20
  14.9 79.1 %all-reduce.13 = bf16[4096,256]{1,0:T(8,128)(2,1)S(1)} all-reduce(f32[4096,256]{1,0:T(8,128)} %fusion.20), channel_id=1, replica_groups=mesh['rows'=64,'panel'=4] {'panel'}, use_global_device_ids=true, to_apply=%region_0.0 | all-reduce | flops 1048576 | bytes 6291456 | tf_op jit(solution)/shard_map/psum | solution.py:26
  94.0 0.0 copy-start.2
  94.0 6.8 fusion.5
  100.8 0.0 all-reduce.8.cloned.1.call-update
  100.8 0.0 all-reduce.10.cloned.1.call-start
  100.9 0.2 copy.8
  101.1 658.6 %all-reduce.8.cloned.1.call-done = f32[1024,256]{0,1:T(8,128)} async-done(((f32[1024,256]{0,1:T(8,128)}), f32[1024,256]{0,1:T(8,128)}) %all-reduce.8.cloned.1.call-update) | async-done | bytes 1048592 | tf_op jit(solution)/shard_map/psum | solution.py:30
  759.6 1.4 convert_add_fusion
  761.1 1.7 fusion.21
  762.8 0.0 all-reduce.10.cloned.1.call-update
  762.8 0.2 all-reduce.12.cloned.1.call-start
  763.1 0.6 convert_reduce_fusion
  763.7 82.8 %all-reduce.10.cloned.1.call-done = f32[256,256]{0,1:T(8,128)} async-done(((f32[256,256]{0,1:T(8,128)}), f32[256,256]{0,1:T(8,128)}) %all-reduce.10.cloned.1.call-update) | async-done | bytes 262160 | tf_op jit(solution)/shard_map/psum | solution.py:31
  846.6 1.1 copy.10
  847.6 1.0 fusion.12
  848.7 11.7 cholesky.50
  860.4 9.8 custom-call.14
  870.2 0.2 constant_dynamic-update-slice_fusion
  870.5 0.3 convolution_subtract_fusion.2
  870.7 11.7 cholesky.105
  882.5 0.6 compare_reduce_fusion
  884.5 0.1 triangular_solve.58
  884.5 4.2 while.1
  884.7 0.6 fusion.39
  885.3 1.4 bitcast_dynamic-update-slice_fusion.2
  886.7 0.6 fusion.39
  887.3 1.4 bitcast_dynamic-update-slice_fusion.2
  888.7 19.7 %custom-call.15 = f32[2,128,128]{1,2,0:T(8,128)S(1)} custom-call(f32[2,128,128]{2,1,0:T(8,128)S(1)} %get-tuple-element.11), custom_call_target="InvertDiagBlocksLowerTriangular" | custom-call | tf_op jit(solution)/shard_map/triangular_solve | solution.py:33
  908.4 0.6 fusion.9
  909.0 0.6 convolution_subtract_fusion.1
  909.6 0.6 fusion.13
  910.2 1.1 pad_maximum_fusion
  911.3 0.9 fusion.18
  912.2 7.7 fusion
  919.9 76.4 %all-reduce.14 = bf16[4096,256]{0,1:T(8,128)(2,1)S(1)} all-reduce(f32[4096,256]{0,1:T(8,128)} %fusion), channel_id=1, replica_groups=mesh['rows'=64,'panel'=4] {'panel'}, use_global_device_ids=true, to_apply=%region_7.8 | all-reduce | flops 1048576 | bytes 6291456 | tf_op jit(solution)/shard_map/psum | solution.py:42
  996.4 0.0 copy-start.1
  996.4 1.4 fusion.1
  997.8 0.6 fusion.22
  998.5 0.0 all-reduce.12.cloned.1.call-update
  998.5 0.8 constant_dynamic-slice_fusion.1
  999.4 157.5 %all-reduce.1 = (f32[256]{0:T(256)S(1)}, f32[]{:T(128)}) all-reduce(f32[256]{0:T(256)S(1)} %bitcast.50, f32[]{:T(128)} %convert_reduce_fusion), channel_id=1, replica_groups=mesh['rows'=64,'panel'=4] {'rows'}, use_global_device_ids=true, to_apply=%region_8.9 | all-reduce | flops 257 | bytes 2056 | tf_op jit(solution)/shard_map/psum | solution.py:43
  1158.1 2.0 copy.12
  1160.2 1.3 copy.11
  1161.5 457.6 %all-reduce.12.cloned.1.call-done = f32[256,256]{1,0:T(8,128)} async-done(((f32[256,256]{1,0:T(8,128)}), f32[256,256]{1,0:T(8,128)}) %all-reduce.12.cloned.1.call-update) | async-done | bytes 262160 | tf_op jit(solution)/shard_map/psum | solution.py:43
  1619.1 2.4 subtract_divide_fusion
  (19 shorter events, 0.2 us)
Async XLA Ops:
  7.2 904.2 %copy-start = (f32[1024]{0:T(1024)S(1)}, f32[1024]{0:T(1024)}, u32[]{:S(2)}) copy-start(f32[1024]{0:T(1024)} %param.6) | copy-start | bytes 12292
  7.2 752.5 %all-reduce.8.cloned.1.call-start = ((), (), s32[]{:S(2)}) async-start(), calls=%async_computation | async-start | bytes 2097152 | tf_op jit(solution)/shard_map/psum | solution.py:30
  94.0 6.8 copy-start.2
  100.8 662.3 %copy-start.3 = (s32[4096]{0:T(1024)S(1)}, s32[4096]{0:T(1024)}, u32[]{:S(2)}) copy-start(s32[4096]{0:T(1024)} %param.7) | copy-start | bytes 49156
  100.8 745.7 %all-reduce.10.cloned.1.call-start = ((), (), s32[]{:S(2)}) async-start(), calls=%async_computation.1 | async-start | bytes 524288 | tf_op jit(solution)/shard_map/psum | solution.py:31
  762.8 856.3 %all-reduce.12.cloned.1.call-start = ((), (), s32[]{:S(2)}) async-start(), calls=%async_computation.2 | async-start | bytes 524288 | tf_op jit(solution)/shard_map/psum | solution.py:43
  996.4 163.8 %copy-start.1 = (f32[1024,256]{0,1:T(8,128)S(1)}, f32[1024,256]{0,1:T(8,128)}, u32[]{:S(2)}) copy-start(f32[1024,256]{0,1:T(8,128)} %pad_maximum_fusion) | copy-start | bytes 3145732
  1161.5 460.0 %copy-start.4 = (f32[256]{0:T(256)}, f32[256]{0:T(256)S(1)}, u32[]{:S(2)}) copy-start(f32[256]{0:T(256)S(1)} %broadcast_divide_fusion) | copy-start | bytes 3076
Sparse Core Ops, SparseCore 0:
  100.9 658.6 all-reduce.7
  762.9 83.5 all-reduce.9
  998.6 620.4 all-reduce.11
where the time goes:
time: 1660 us; the launch traced here: 1630 us
  waiting for transfers between devices  1200 us (72%)
  blocking collectives  313 us (19%)
  other arithmetic  60.1 us (4%)
  matrix products  29.2 us (2%)
    psum x1, waiting for transfers between devices, per_device(): lax.psum(cross_term, 'rows') / jnp.float32(rows_total)  659 us
    psum x1, waiting for transfers between devices, per_device(): totals = lax.psum(moments_of(score_half, mask), 'rows')  458 us
    psum x1, blocking collectives, per_device(): totals = lax.psum(moments_of(score_half, mask), 'rows')  158 us
    psum x1, waiting for transfers between devices, per_device(): gram_matrix = lax.psum(jnp.dot(crossed.T, crossed, precision=high), 'panel')  82.8 us
    psum x1, blocking collectives, per_device(): projected = lax.psum(partial_proj, 'panel').astype(jnp.bfloat16)  79.1 us
    psum x1, blocking collectives, per_device(): score_half = lax.psum(score_part, 'panel').astype(jnp.bfloat16)  76.4 us
    another operation x6, other arithmetic, per_device(): factor = jnp.linalg.cholesky(gram_matrix)  34 us
  transfers between devices with their start and end apart: 3, of which 3 were waited for; matrix products, arithmetic and copies ran while one was open for 0% of the time, Pallas kernels for 0%

commit v1 on v0

v1 whole, which is shorter than its diff:
```python
import functools

import jax
import jax.numpy as jnp
from jax import lax
from jax.experimental import pallas as pl
from jax.experimental.pallas import tpu as pltpu
from jax.sharding import PartitionSpec as P

MESH = pl.DeviceIdType.MESH
F32 = jnp.float32
BF16 = jnp.bfloat16
CHUNK = 256
NZ, NY, NXH = 8, 4, 2
ROW_CONTRACT = (((0,), (0,)), ((), ()))
LANE_CONTRACT = (((1,), (1,)), ((), ()))
PLAIN = (((1,), (0,)), ((), ()))


def where_am_i():
    r = lax.axis_index("rows")
    p = lax.axis_index("panel")
    z, y, xh = lax.div(r, NY * NXH), lax.rem(lax.div(r, NXH), NY), lax.rem(r, NXH)
    return z, y, xh, lax.div(p, 2), lax.rem(p, 2)


def device(z, y, xh, xl, core):
    return (z * (NY * NXH) + y * NXH + xh, xl * 2 + core)


def remote(src, dst, send_sem, recv_sem, dev):
    return pltpu.make_async_remote_copy(
        src_ref=src, dst_ref=dst, send_sem=send_sem, recv_sem=recv_sem, device_id=dev, device_id_type=MESH
    )


def loop(count, start=0):
    def run(body):
        lax.fori_loop(start, count, lambda i, c: (body(i), c)[1], 0)

    return run


def rows_of(block, size):
    return pl.ds(pl.multiple_of(block * size, size), size)


LEAF = 64


def leaf_inverse(a):
    n = a.shape[0]
    tiles = n // 8
    lane = lax.broadcasted_iota(jnp.int32, (n, n), 1)
    row = lax.broadcasted_iota(jnp.int32, (n, n), 0)
    whole = jnp.concatenate([a, jnp.where(lane == row, 1.0, 0.0)], axis=1)
    m = [whole[8 * t : 8 * t + 8, :] for t in range(tiles)]
    shape = m[0].shape
    sub = lax.broadcasted_iota(jnp.int32, shape, 0)
    out = []
    for t0 in range(tiles):
        diag = jnp.ones(shape, F32)
        cols = [
            [jnp.broadcast_to(m[t][:, k : k + 1], shape) for t in range(t0, tiles)]
            for k in range(8 * t0, 8 * t0 + 8)
        ]
        for s in range(8):
            pivot = jnp.broadcast_to(cols[s][0][s : s + 1, :], shape)
            diag = jnp.where(sub == s, pivot, diag)
            inverse = 1.0 / pivot
            prow = jnp.broadcast_to(m[t0][s : s + 1, :], shape)
            heads = [jnp.broadcast_to(cols[c][0][s : s + 1, :], shape) for c in range(s + 1, 8)]
            for t in range(t0, tiles):
                f = cols[s][t - t0] * inverse
                if t == t0:
                    f = jnp.where(sub > s, f, 0.0)
                m[t] = m[t] - f * prow
                for c in range(s + 1, 8):
                    cols[c][t - t0] = cols[c][t - t0] - f * heads[c - s - 1]
        r = lax.rsqrt(diag)
        r = r * (1.5 - 0.5 * diag * r * r)
        out.append(m[t0] * r)
    return jnp.concatenate(out, axis=0)[:, n:]


def dot32(a, b, dims):
    return lax.dot_general(a, b, dims, precision=lax.Precision.HIGHEST, preferred_element_type=F32)


def factor_inverse(a):
    n = a.shape[0]
    if n == LEAF:
        return leaf_inverse(a)
    h = n // 2
    w11 = factor_inverse(a[:h, :h])
    l21 = dot32(a[h:, :h], w11, LANE_CONTRACT)
    w22 = factor_inverse(a[h:, h:] - dot32(l21, l21, LANE_CONTRACT))
    w21 = -dot32(dot32(w22, l21, PLAIN), w11, PLAIN)
    upper = jnp.concatenate([w11, jnp.zeros((h, h), F32)], axis=1)
    return jnp.concatenate([upper, jnp.concatenate([w21, w22], axis=1)], axis=0)


def ortho_kernel(gram_ref, hi_ref, lo_ref, ortho_ref, half_ref):
    inverse = factor_inverse(gram_ref[...])
    w_hi = inverse.astype(BF16)
    w_lo = (inverse - w_hi.astype(F32)).astype(BF16)
    dims = (((0,), (1,)), ((), ()))
    for j in range(NY):
        hi, lo = hi_ref[j], lo_ref[j]
        q = lax.dot_general(hi, w_lo, dims, preferred_element_type=F32)
        q += lax.dot_general(lo, w_hi, dims, preferred_element_type=F32)
        q += lax.dot_general(hi, w_hi, dims, preferred_element_type=F32)
        ortho_ref[j * 256 : (j + 1) * 256, :] = q
        half_ref[j * 256 : (j + 1) * 256, :] = q.astype(BF16)


def ortho_call(gram, hi, lo):
    k = gram.shape[0]
    cols = NY * 256
    return pl.pallas_call(
        ortho_kernel,
        out_shape=(jax.ShapeDtypeStruct((cols, k), F32), jax.ShapeDtypeStruct((cols, k), BF16)),
        in_specs=[pl.BlockSpec(memory_space=pltpu.VMEM)] * 3,
        out_specs=(pl.BlockSpec(memory_space=pltpu.VMEM),) * 2,
        name="orthonormalise",
    )(gram, hi, lo)


def cross_kernel(
    rows_total, acts_hbm, basis_ref, hi_ref, lo_ref, gram_ref,
    acts, tosib, fromsib, own, cout, cin, total, acc, ysend, yrecv, s32, zsend, zrecv, bt, ct,
    g, gsib, gx, gc, gtot,
    ld, sib_s, sib_r, c_s, c_r, t_s, t_r, y_s, y_r, z_s, z_r, az_s, az_r, ay_s, ay_r, g_s, g_r,
):
    z, y, xh, xl, core = where_am_i()
    zx = z * NXH + xh
    nzx = NZ * NXH
    chunks = acts.shape[0] // CHUNK // 2
    sibling = device(z, y, xh, xl, 1 - core)
    across = device(z, y, xh, 1 - xl, core)

    def ypeer(d):
        q = lax.rem(y + d, NY)
        return q, device(z, q, xh, xl, core)

    def zpeer(d):
        q = lax.rem(zx + d, nzx)
        return q, device(lax.div(q, NXH), y, lax.rem(q, NXH), xl, core)

    def load(k):
        at = rows_of(k, CHUNK)
        return pltpu.make_async_copy(acts_hbm.at[at, :], acts.at[at, :], ld.at[k])

    their, mine = (1 - core) * chunks, core * chunks

    @loop(chunks)
    def _(i):
        load(their + i).start()

    @loop(chunks)
    def _(i):
        load(mine + i).start()

    barrier = pltpu.get_barrier_semaphore()
    for dev in (sibling, across):
        pl.semaphore_signal(barrier, inc=1, device_id=dev, device_id_type=MESH)

    @loop(NY, 1)
    def _(d):
        pl.semaphore_signal(barrier, inc=1, device_id=ypeer(d)[1], device_id_type=MESH)

    @loop(nzx, 1)
    def _(d):
        pl.semaphore_signal(barrier, inc=1, device_id=zpeer(d)[1], device_id_type=MESH)

    @loop(chunks)
    def _(i):
        load(their + i).wait()
        tosib[i] = jnp.dot(
            acts[rows_of(their + i, CHUNK), :], basis_ref[...], preferred_element_type=F32
        ).astype(BF16)

    pl.semaphore_wait(barrier, 2 + (NY - 1) + (nzx - 1))

    def sib_copy(i):
        return remote(tosib.at[i], fromsib.at[i], sib_s.at[i], sib_r.at[i], sibling)

    def c_copy(i):
        return remote(cout.at[i], cin.at[i], c_s.at[i], c_r.at[i], across)

    def t_copy(i, half):
        return remote(total.at[half, i], total.at[half, i], t_s.at[i], t_r.at[i], sibling)

    @loop(chunks)
    def _(i):
        sib_copy(i).start()

    @loop(chunks)
    def _(i):
        load(mine + i).wait()
        part = jnp.dot(acts[rows_of(mine + i, CHUNK), :], basis_ref[...], preferred_element_type=F32)
        sib_copy(i).wait_recv()
        part = part + fromsib[i].astype(F32)
        own[i] = part
        cout[i] = part.astype(BF16)
        c_copy(i).start()

    bt[...] = basis_ref[rows_of(y, 256), :].astype(F32).T.reshape(bt.shape)
    acc[...] = jnp.zeros_like(acc)

    def add_terms(tot, k):
        for j in range(NY):
            acc[j] += lax.dot_general(
                tot, acts[rows_of(k, CHUNK), j * 256 : (j + 1) * 256], ROW_CONTRACT, preferred_element_type=F32
            )

    @loop(chunks)
    def _(i):
        c_copy(i).wait_recv()
        tot = (own[i] + cin[i].astype(F32)).astype(BF16)
        total[core, i] = tot
        t_copy(i, core).start()
        add_terms(tot, mine + i)
        t_copy(i, 1 - core).wait_recv()
        add_terms(total[1 - core, i], their + i)

    ysend[...] = acc[...].astype(BF16)

    def y_copy(d):
        q, dev = ypeer(d)
        return remote(ysend.at[q], yrecv.at[d], y_s.at[d], y_r.at[d], dev)

    @loop(NY, 1)
    def _(d):
        y_copy(d).start()

    s32[...] = acc[y].reshape(s32.shape)

    @loop(NY, 1)
    def _(d):
        y_copy(d).wait_recv()
        s32[...] += yrecv[d].astype(F32).reshape(s32.shape)

    zsend[...] = s32[...].astype(BF16)

    def z_copy(d):
        q, dev = zpeer(d)
        return remote(zsend.at[q], zrecv.at[d], z_s.at[d], z_r.at[d], dev)

    @loop(nzx, 1)
    def _(d):
        z_copy(d).start()

    def add_z(d, s):
        z_copy(d).wait_recv()
        return s + zrecv[d].astype(F32)

    block = lax.fori_loop(1, nzx, add_z, s32[zx])
    block = block / F32(rows_total) + bt[zx]
    upper = block.astype(BF16)
    ct[0, y, zx] = upper
    ct[1, y, zx] = (block - upper.astype(F32)).astype(BF16)

    def az_copy(d, part):
        at = ct.at[part, y, zx]
        return remote(at, at, az_s.at[part, d], az_r.at[part, d], zpeer(d)[1])

    def ay_copy(d, part):
        at = ct.at[part, y]
        return remote(at, at, ay_s.at[part, d], ay_r.at[part, d], ypeer(d)[1])

    for part in range(2):

        @loop(nzx, 1)
        def _(d, part=part):
            az_copy(d, part).start()

    for part in range(2):

        @loop(nzx, 1)
        def _(d, part=part):
            az_copy(d, part).wait_recv()

        @loop(NY, 1)
        def _(d, part=part):
            ay_copy(d, part).start()

    @loop(NY, 1)
    def _(d):
        ay_copy(d, 0).wait_recv()

    gram = jnp.zeros((256, 256), F32)
    for j in range(NY):
        piece = ct[0, j].reshape(256, 256)
        gram += lax.dot_general(piece, piece, LANE_CONTRACT, preferred_element_type=F32)
    g[...] = gram.reshape(g.shape)
    first = remote(g, gsib, g_s.at[0], g_r.at[0], sibling)
    first.start()
    hi_ref[...] = ct[0].reshape(hi_ref.shape)
    first.wait_recv()
    gx[...] = g[...] + gsib[...]
    second = remote(gx.at[core], gc, g_s.at[1], g_r.at[1], across)
    second.start()
    second.wait_recv()
    gtot[core] = gx[core] + gc[...]
    third = remote(gtot.at[core], gtot.at[core], g_s.at[2], g_r.at[2], sibling)
    third.start()
    third.wait_recv()
    gram_ref[...] = gtot[...].reshape(256, 256)

    @loop(NY, 1)
    def _(d):
        ay_copy(d, 1).wait_recv()

    lo_ref[...] = ct[1].reshape(lo_ref.shape)

    @loop(chunks)
    def _(i):
        sib_copy(i).wait_send()
        c_copy(i).wait_send()
        t_copy(i, core).wait_send()

    @loop(NY, 1)
    def _(d):
        y_copy(d).wait_send()
        ay_copy(d, 0).wait_send()
        ay_copy(d, 1).wait_send()

    @loop(nzx, 1)
    def _(d):
        z_copy(d).wait_send()
        az_copy(d, 0).wait_send()
        az_copy(d, 1).wait_send()

    first.wait_send()
    second.wait_send()
    third.wait_send()


def cross_call(acts, basis, rows_total):
    rows, cols = acts.shape
    k = basis.shape[1]
    chunks = rows // CHUNK // 2
    nzx = NZ * NXH
    dma = pltpu.SemaphoreType.DMA
    vm = pltpu.VMEM
    return pl.pallas_call(
        functools.partial(cross_kernel, rows_total),
        out_shape=(jax.ShapeDtypeStruct((NY, k, 256), BF16),) * 2 + (jax.ShapeDtypeStruct((k, k), F32),),
        in_specs=[pl.BlockSpec(memory_space=pl.ANY), pl.BlockSpec(memory_space=vm)],
        out_specs=(pl.BlockSpec(memory_space=vm),) * 3,
        scratch_shapes=[
            vm((rows, cols), BF16),
            vm((chunks, CHUNK, k), BF16),
            vm((chunks, CHUNK, k), BF16),
            vm((chunks, CHUNK, k), F32),
            vm((chunks, CHUNK, k), BF16),
            vm((chunks, CHUNK, k), BF16),
            vm((2, chunks, CHUNK, k), BF16),
            vm((NY, k, 256), F32),
            vm((NY, k, 256), BF16),
            vm((NY, k, 256), BF16),
            vm((nzx, k // nzx, 256), F32),
            vm((nzx, k // nzx, 256), BF16),
            vm((nzx, k // nzx, 256), BF16),
            vm((nzx, k // nzx, 256), F32),
            vm((2, NY, nzx, k // nzx, 256), BF16),
            vm((2, k // 2, k), F32),
            vm((2, k // 2, k), F32),
            vm((2, k // 2, k), F32),
            vm((k // 2, k), F32),
            vm((2, k // 2, k), F32),
            dma((2 * chunks,)),
        ]
        + [dma((chunks,))] * 6
        + [dma((NY,))] * 2
        + [dma((nzx,))] * 2
        + [dma((2, nzx))] * 2
        + [dma((2, NY))] * 2
        + [dma((3,))] * 2,
        compiler_params=pltpu.CompilerParams(collective_id=0, has_side_effects=True),
        name="cross_terms",
    )(acts, basis)


def score_kernel(
    acts_hbm, ortho_ref, offset_ref, mask_ref, scores_ref, mean_ref, cov_ref,
    acts, tosib, fromsib, cout, cin, mine, sc, mom, mrecv, hsum, xrecv, zbuf, fin,
    ld, sib_s, sib_r, c_s, c_r, m_s, m_r, x_s, x_r, zz_s, zz_r, ax_s, ax_r,
):
    z, y, xh, xl, core = where_am_i()
    x = xh * 2 + xl
    xy = x * NY + y
    nxy = 4 * NY
    quarter = acts.shape[0] // 4
    chunks = quarter // CHUNK
    sibling = device(z, y, xh, xl, 1 - core)
    across = device(z, y, xh, 1 - xl, core)

    def xypeer(d):
        q = lax.rem(xy + d, nxy)
        px = lax.div(q, NY)
        return q, device(z, lax.rem(q, NY), lax.div(px, 2), lax.rem(px, 2), core)

    def zpeer(d):
        return device(lax.rem(z + d, NZ), y, xh, xl, core)

    def load(k):
        at = rows_of(k, CHUNK)
        return pltpu.make_async_copy(acts_hbm.at[at, :], acts.at[at, :], ld.at[k])

    def first_chunk(there, c):
        return ((xl + there - 2 * xl * there) * 2 + c) * chunks

    order = [(1, 1 - core, 0), (0, 1 - core, 1), (1, core, 0), (0, core, 1)]
    for there, c, _ in order:

        @loop(chunks)
        def _(i, there=there, c=c):
            load(first_chunk(there, c) + i).start()

    barrier = pltpu.get_barrier_semaphore()
    pl.semaphore_signal(barrier, inc=1, device_id=sibling, device_id_type=MESH)

    @loop(nxy, 1)
    def _(d):
        pl.semaphore_signal(barrier, inc=1, device_id=xypeer(d)[1], device_id_type=MESH)

    @loop(NZ, 1)
    def _(d):
        pl.semaphore_signal(barrier, inc=1, device_id=zpeer(d), device_id_type=MESH)

    def part_of(k):
        load(k).wait()
        return jnp.dot(acts[rows_of(k, CHUNK), :], ortho_ref[...], preferred_element_type=F32) - offset_ref[...]

    for there, slot in ((1, 0), (0, 1)):

        @loop(chunks)
        def _(i, there=there, slot=slot):
            tosib[slot, i] = part_of(first_chunk(there, 1 - core) + i).astype(BF16)

    pl.semaphore_wait(barrier, 1 + (nxy - 1) + (NZ - 1))

    def sib_copy(slot, i):
        return remote(tosib.at[slot, i], fromsib.at[slot, i], sib_s.at[slot, i], sib_r.at[slot, i], sibling)

    def c_copy(i):
        return remote(cout.at[i], cin.at[i], c_s.at[i], c_r.at[i], across)

    for slot in range(2):

        @loop(chunks)
        def _(i, slot=slot):
            sib_copy(slot, i).start()

    @loop(chunks)
    def _(i):
        part = part_of(first_chunk(1, core) + i)
        sib_copy(0, i).wait_recv()
        cout[i] = (part + fromsib[0, i].astype(F32)).astype(BF16)
        c_copy(i).start()

    @loop(chunks)
    def _(i):
        part = part_of(first_chunk(0, core) + i)
        sib_copy(1, i).wait_recv()
        mine[i] = part + fromsib[1, i].astype(F32)

    second = jnp.zeros((256, 256), F32)
    first = jnp.zeros((256, 128), F32)
    ones = jnp.ones((CHUNK, 128), BF16)
    base = pl.multiple_of((xl * 2 + core) * quarter, quarter)
    for i in range(chunks):
        c_copy(i).wait_recv()
        score = (mine[i] + cin[i].astype(F32)).astype(BF16)
        sc[i] = score
        weight = mask_ref[:, pl.ds(pl.multiple_of(base + i * CHUNK, CHUNK), CHUNK)].astype(F32)
        chosen = (score.astype(F32).T * weight).astype(BF16)
        second += jnp.dot(chosen, score, preferred_element_type=F32)
        first += jnp.dot(chosen, ones, preferred_element_type=F32)
    count = jnp.sum(mask_ref[:, pl.ds(base, quarter)].astype(F32), keepdims=True)
    lane = lax.broadcasted_iota(jnp.int32, first.shape, 1)
    side = jnp.where(lane == 1, count, first)
    mom[:, :, :, 0:256] = second.reshape(2, nxy, 8, 256)
    mom[:, :, :, 256:384] = side.reshape(2, nxy, 8, 128)
    scores_ref[...] = sc[...].reshape(scores_ref.shape)

    halves = remote(mom.at[1 - core], mrecv, m_s.at[0], m_r.at[0], sibling)
    halves.start()
    halves.wait_recv()
    hsum[...] = mom[core] + mrecv[...]

    def x_copy(d):
        q, dev = xypeer(d)
        return remote(hsum.at[q], xrecv.at[d], x_s.at[d], x_r.at[d], dev)

    @loop(nxy, 1)
    def _(d):
        x_copy(d).start()

    def add_x(d, s):
        x_copy(d).wait_recv()
        return s + xrecv[d]

    zbuf[z] = lax.fori_loop(1, nxy, add_x, hsum[xy])

    def zz_copy(d):
        return remote(zbuf.at[z], zbuf.at[z], zz_s.at[d], zz_r.at[d], zpeer(d))

    @loop(NZ, 1)
    def _(d):
        zz_copy(d).start()

    @loop(NZ, 1)
    def _(d):
        zz_copy(d).wait_recv()

    tot = zbuf[0]
    for d in range(1, NZ):
        tot = tot + zbuf[d]
    fin[core, xy] = tot

    def ax_copy(d):
        return remote(fin.at[core, xy], fin.at[core, xy], ax_s.at[d], ax_r.at[d], xypeer(d)[1])

    @loop(nxy, 1)
    def _(d):
        ax_copy(d).start()

    @loop(nxy, 1)
    def _(d):
        ax_copy(d).wait_recv()

    whole = remote(fin.at[core], fin.at[core], m_s.at[1], m_r.at[1], sibling)
    whole.start()
    whole.wait_recv()

    second = fin[:, :, :, 0:256].reshape(256, 256)
    side = fin[:, :, :, 256:384].reshape(256, 128)
    weight_sum = side[0:1, 1:2]
    mean = side / jnp.maximum(weight_sum, 1.0)
    mean_row = mean.T[0:1, :]
    mean_ref[...] = mean_row
    cov_ref[...] = (second - weight_sum * (mean[:, 0:1] * mean_row)) / jnp.maximum(weight_sum - 1.0, 1.0)

    for slot in range(2):

        @loop(chunks)
        def _(i, slot=slot):
            sib_copy(slot, i).wait_send()

    @loop(chunks)
    def _(i):
        c_copy(i).wait_send()

    halves.wait_send()
    whole.wait_send()

    @loop(nxy, 1)
    def _(d):
        x_copy(d).wait_send()
        ax_copy(d).wait_send()

    @loop(NZ, 1)
    def _(d):
        zz_copy(d).wait_send()


def score_call(acts, ortho_half, offset_part, mask):
    rows, cols = acts.shape
    k = ortho_half.shape[1]
    chunks = rows // 4 // CHUNK
    nxy = 4 * NY
    dma = pltpu.SemaphoreType.DMA
    vm = pltpu.VMEM
    return pl.pallas_call(
        score_kernel,
        out_shape=(
            jax.ShapeDtypeStruct((rows // 4, k), BF16),
            jax.ShapeDtypeStruct((1, k), F32),
            jax.ShapeDtypeStruct((k, k), F32),
        ),
        in_specs=[pl.BlockSpec(memory_space=pl.ANY)] + [pl.BlockSpec(memory_space=vm)] * 3,
        out_specs=(pl.BlockSpec(memory_space=vm),) * 3,
        scratch_shapes=[
            vm((rows, cols), BF16),
            vm((2, chunks, CHUNK, k), BF16),
            vm((2, chunks, CHUNK, k), BF16),
            vm((chunks, CHUNK, k), BF16),
            vm((chunks, CHUNK, k), BF16),
            vm((chunks, CHUNK, k), F32),
            vm((chunks, CHUNK, k), BF16),
            vm((2, nxy, 8, k + 128), F32),
            vm((nxy, 8, k + 128), F32),
            vm((nxy, 8, k + 128), F32),
            vm((nxy, 8, k + 128), F32),
            vm((NZ, 8, k + 128), F32),
            vm((2, nxy, 8, k + 128), F32),
            dma((4 * chunks,)),
            dma((2, chunks)),
            dma((2, chunks)),
            dma((chunks,)),
            dma((chunks,)),
            dma((2,)),
            dma((2,)),
            dma((nxy,)),
            dma((nxy,)),
            dma((NZ,)),
            dma((NZ,)),
            dma((nxy,)),
            dma((nxy,)),
        ],
        compiler_params=pltpu.CompilerParams(collective_id=1, has_side_effects=True),
        name="scores_and_moments",
    )(acts, ortho_half, offset_part, mask)


def per_device(acts, basis, center, mask):
    high = lax.Precision.HIGHEST
    rows_total = acts.shape[0] * lax.axis_size("rows")
    hi, lo, gram_matrix = cross_call(acts, basis, rows_total)
    orthonormal, ortho_half = ortho_call(gram_matrix, hi, lo)
    offset_part = jnp.dot(center[None, :], orthonormal, precision=high)
    scores, mean, cov = score_call(acts, ortho_half, offset_part, mask[None, :])
    return (orthonormal, scores, mean.reshape(-1), cov)


def solution(mesh):
    placed = (P("rows", "panel"), P("panel", None), P("panel"), P("rows"))
    return jax.shard_map(
        per_device,
        mesh=mesh,
        in_specs=placed,
        out_specs=(P("panel", None), P(("rows", "panel"), None), P(), P()),
        check_vma=False,
    )
```

time: 1660 us -> 145 us (0.09); the launches traced: 1630 us -> 144 us
  waiting for transfers between devices: 1200 us -> 0 us
  blocking collectives: 313 us -> 0 us
  Pallas kernels: 0 us -> 136 us
  other arithmetic: 60.1 us -> 0 us
  matrix products: 29.2 us -> 2.38 us
    psum x3 -> x0, waiting for transfers between devices: 1200 us -> none  [the longest x1 659 us: per_device(): lax.psum(cross_term, 'rows') / jnp.float32(rows_total)]
    psum x3 -> x0, blocking collectives: 313 us -> none  [the longest x1 158 us: per_device(): totals = lax.psum(moments_of(score_half, mask), 'rows')]
    pallas_call x0 -> x3, Pallas kernels: none -> 136 us  [the longest x1 81.9 us: cross_call(): pl.pallas_call(functools.partial(cross_kernel, rows_total), out_shape=(ja...]
    another operation x10 -> x0, other arithmetic: 54.7 us -> none  [the longest x6 34 us: per_device(): factor = jnp.linalg.cholesky(gram_matrix)]
    dot_general x7 -> x1, matrix products: 26.9 us -> 2.38 us  [per_device(): offset_part = jnp.dot(center[None, :], orthonormal, precision=high)]
  transfers between devices with their start and end apart: 3 -> 0, of which waited for: 3 -> 0; matrix products, arithmetic and copies ran while one was open for 0% -> 0% of each run, Pallas kernels for 0% -> 0%
where the time goes in v1:
time: 145 us; the launch traced here: 144 us
  Pallas kernels  136 us (94%)
  local copies, waits for them, and re-layouts  5.42 us (4%)
  matrix products  2.38 us (2%)
    pallas_call x1, Pallas kernels, cross_call(): pl.pallas_call(functools.partial(cross_kernel, rows_total), out_shape=(ja...  81.9 us
    pallas_call x1, Pallas kernels, score_call(): pl.pallas_call(score_kernel, out_shape=(jax.ShapeDtypeStruct((rows // 4,...  40.5 us
    pallas_call x1, Pallas kernels, ortho_call(): pl.pallas_call(ortho_kernel, out_shape=(jax.ShapeDtypeStruct((cols, k), F...  13.5 us
    unnamed x5, local copies, waits for them, and re-layouts  5.42 us

profile of v1, /device:TPU:1, one launch (start us, length us, event | category | flops | bytes accessed | tf_op | source)
XLA Modules:
  0.0 144.3 jit_solution(2117019604070169205)
XLA Ops:
  0.6 0.0 copy-start
  0.6 0.7 copy-done
  1.3 81.9 %cross_terms.1 = (bf16[4,256,256]{2,1,0:T(8,128)(2,1)}, bf16[4,256,256]{2,1,0:T(8,128)(2,1)}, f32[256,256]{1,0:T(8,128)}) custom-call(bf16[4096,1024]{1,0:T(8,128)(2,1)} %acts_hbm.3, bf16[1024,256]{1,0:T(8,128)(2,1)} %basis_ref.1), custom_call_target="tpu_custom_call" | custom-call | tf_op jit(solution)/shard_map/cross_terms/pallas_call | solution.py:347
  83.2 13.5 %orthonormalise.1 = (f32[1024,256]{1,0:T(8,128)}, bf16[1024,256]{1,0:T(8,128)(2,1)}) custom-call(f32[256,256]{1,0:T(8,128)} %get-tuple-element.12.gram_ref, bf16[4,256,256]{2,1,0:T(8,128)(2,1)} %get-tuple-element.13.hi_ref, bf16[4,256,256]{2,1,0:T(8,128)(2,1)} %get-tuple-element.14.lo_ref), custom_call_target="tpu_custom_call" | custom-call | tf_op jit(solution)/shard_map/orthonormalise/pallas_call | solution.py:120
  96.7 2.4 %fusion.offset_ref = f32[1,256]{1,0:T(1,128)} fusion(f32[1024,256]{1,0:T(8,128)} %get-tuple-element.24, f32[1024,1]{0,1:T(1,128)S(1)} %bitcast.6), kind=kOutput, calls=%fused_computation | convolution fusion | flops 3145728 | bytes 1053696 | tf_op jit(solution)/shard_map/dot_general | solution.py:624
  99.1 40.5 %scores_and_moments.1 = (bf16[1024,256]{1,0:T(8,128)(2,1)}, f32[1,256]{1,0:T(1,128)}, f32[256,256]{1,0:T(8,128)}) custom-call(bf16[4096,1024]{1,0:T(8,128)(2,1)} %acts_hbm.3, bf16[1024,256]{1,0:T(8,128)(2,1)} %get-tuple-element.16.ortho_ref, f32[1,256]{1,0:T(1,128)} %fusion.offset_ref, s32[1,4096]{1,0:T(1,128)} %bitcast.7), custom_call_target="tpu_custom_call" | custom-call | tf_op jit(solution)/shard_map/scores_and_moments/pallas_call | solution.py:577
  139.6 1.9 %copy.11 = bf16[1024,256]{1,0:T(8,128)(2,1)} copy(bf16[1024,256]{1,0:T(8,128)(2,1)} %get-tuple-element.25) | data formatting | bytes 1048576
  141.4 1.2 copy.12
  142.6 1.7 %copy.13 = f32[256,256]{1,0:T(8,128)} copy(f32[256,256]{1,0:T(8,128)} %get-tuple-element.27) | data formatting | bytes 524288
Async XLA Ops:
  0.6 0.7 copy-start

commit v2 on v0

v2 whole, which is shorter than its diff:
```python
import functools

import jax
import jax.numpy as jnp
from jax import lax
from jax.experimental import pallas as pl
from jax.experimental.pallas import tpu as pltpu
from jax.sharding import PartitionSpec as P

MESH = pl.DeviceIdType.MESH
F32 = jnp.float32
BF16 = jnp.bfloat16
CHUNK = 256
NZ, NY, NXH = 8, 4, 2
HALF = 128
ROW_CONTRACT = (((0,), (0,)), ((), ()))
LANE_CONTRACT = (((1,), (1,)), ((), ()))
PLAIN = (((1,), (0,)), ((), ()))


def where_am_i():
    r = lax.axis_index("rows")
    p = lax.axis_index("panel")
    z, y, xh = lax.div(r, NY * NXH), lax.rem(lax.div(r, NXH), NY), lax.rem(r, NXH)
    return z, y, xh, lax.div(p, 2), lax.rem(p, 2)


def device(z, y, xh, xl, core):
    return (z * (NY * NXH) + y * NXH + xh, xl * 2 + core)


def remote(src, dst, send_sem, recv_sem, dev):
    return pltpu.make_async_remote_copy(
        src_ref=src, dst_ref=dst, send_sem=send_sem, recv_sem=recv_sem, device_id=dev, device_id_type=MESH
    )


def loop(count, start=0):
    def run(body):
        lax.fori_loop(start, count, lambda i, c: (body(i), c)[1], 0)

    return run


def rows_of(block, size):
    return pl.ds(pl.multiple_of(block * size, size), size)


LEAF = 64


def leaf_inverse(a):
    n = a.shape[0]
    tiles = n // 8
    lane = lax.broadcasted_iota(jnp.int32, (n, n), 1)
    row = lax.broadcasted_iota(jnp.int32, (n, n), 0)
    whole = jnp.concatenate([a, jnp.where(lane == row, 1.0, 0.0)], axis=1)
    m = [whole[8 * t : 8 * t + 8, :] for t in range(tiles)]
    shape = m[0].shape
    sub = lax.broadcasted_iota(jnp.int32, shape, 0)
    out = []
    for t0 in range(tiles):
        diag = jnp.ones(shape, F32)
        cols = [
            [jnp.broadcast_to(m[t][:, k : k + 1], shape) for t in range(t0, tiles)]
            for k in range(8 * t0, 8 * t0 + 8)
        ]
        for s in range(8):
            pivot = jnp.broadcast_to(cols[s][0][s : s + 1, :], shape)
            diag = jnp.where(sub == s, pivot, diag)
            inverse = 1.0 / pivot
            prow = jnp.broadcast_to(m[t0][s : s + 1, :], shape)
            heads = [jnp.broadcast_to(cols[c][0][s : s + 1, :], shape) for c in range(s + 1, 8)]
            for t in range(t0, tiles):
                f = cols[s][t - t0] * inverse
                if t == t0:
                    f = jnp.where(sub > s, f, 0.0)
                m[t] = m[t] - f * prow
                for c in range(s + 1, 8):
                    cols[c][t - t0] = cols[c][t - t0] - f * heads[c - s - 1]
        r = lax.rsqrt(diag)
        r = r * (1.5 - 0.5 * diag * r * r)
        out.append(m[t0] * r)
    return jnp.concatenate(out, axis=0)[:, n:]


def dot32(a, b, dims):
    return lax.dot_general(a, b, dims, precision=lax.Precision.HIGHEST, preferred_element_type=F32)


def factor_inverse(a):
    n = a.shape[0]
    if n == LEAF:
        return leaf_inverse(a)
    h = n // 2
    w11 = factor_inverse(a[:h, :h])
    l21 = dot32(a[h:, :h], w11, LANE_CONTRACT)
    w22 = factor_inverse(a[h:, h:] - dot32(l21, l21, LANE_CONTRACT))
    w21 = -dot32(dot32(w22, l21, PLAIN), w11, PLAIN)
    upper = jnp.concatenate([w11, jnp.zeros((h, h), F32)], axis=1)
    return jnp.concatenate([upper, jnp.concatenate([w21, w22], axis=1)], axis=0)


def step_kernel(
    rows_total, acts_hbm, basis_ref, center_ref, mask_ref, ortho_ref, scores_ref, moments_ref,
    acts, tosib, fromsib, own, cout, cin, total, acc, ysend, yrecv, s32, zsend, zrecv, bt, ct,
    g, gsib, gx, gc, gtot, qb, ptosib, pfromsib, pout, pin, mine32, mom, mrecv, hsum, xrecv, zbuf, fin,
    ld, sib_s, sib_r, c_s, c_r, t_s, t_r, y_s, y_r, z_s, z_r, az_s, az_r, ay_s, ay_r, g_s, g_r,
    p_s, p_r, pc_s, pc_r, m_s, m_r, x_s, x_r, zz_s, zz_r, ax_s, ax_r,
):
    z, y, xh, xl, core = where_am_i()
    zx = xh * NZ + z
    nzx = NZ * NXH
    x = xh * 2 + xl
    xy = x * NY + y
    nxy = 4 * NY
    chunks = acts.shape[0] // CHUNK // 2
    quarter = acts.shape[0] // 4
    qchunks = quarter // CHUNK
    sibling = device(z, y, xh, xl, 1 - core)
    across = device(z, y, xh, 1 - xl, core)

    def ypeer(d):
        q = lax.rem(y + d, NY)
        return q, device(z, q, xh, xl, core)

    def zxpeer(d):
        q = lax.rem(zx + d, nzx)
        return q, device(lax.rem(q, NZ), y, lax.div(q, NZ), xl, core)

    def xypeer(d):
        q = lax.rem(xy + d, nxy)
        px = lax.div(q, NY)
        return q, device(z, lax.rem(q, NY), lax.div(px, 2), lax.rem(px, 2), core)

    def zpeer(d):
        return device(lax.rem(z + d, NZ), y, xh, xl, core)

    def load(k):
        at = rows_of(k, CHUNK)
        return pltpu.make_async_copy(acts_hbm.at[at, :], acts.at[at, :], ld.at[k])

    their, mine = (1 - core) * chunks, core * chunks

    @loop(chunks)
    def _(i):
        load(their + i).start()

    @loop(chunks)
    def _(i):
        load(mine + i).start()

    barrier = pltpu.get_barrier_semaphore()
    pl.semaphore_signal(barrier, inc=1, device_id=sibling, device_id_type=MESH)

    @loop(NY, 1)
    def _(d):
        pl.semaphore_signal(barrier, inc=1, device_id=ypeer(d)[1], device_id_type=MESH)

    @loop(nzx, 1)
    def _(d):
        pl.semaphore_signal(barrier, inc=1, device_id=zxpeer(d)[1], device_id_type=MESH)

    @loop(nxy, 1)
    def _(d):
        pl.semaphore_signal(barrier, inc=1, device_id=xypeer(d)[1], device_id_type=MESH)

    def project(k):
        load(k).wait()
        return jnp.dot(acts[rows_of(k, CHUNK), :], basis_ref[...], preferred_element_type=F32)

    @loop(chunks)
    def _(i):
        tosib[i] = project(their + i).astype(BF16)

    @loop(chunks)
    def _(i):
        own[i] = project(mine + i)

    pl.semaphore_wait(barrier, 1 + (NY - 1) + (nzx - 1) + (nxy - 1))

    def sib_copy(i):
        return remote(tosib.at[i], fromsib.at[i], sib_s.at[i], sib_r.at[i], sibling)

    def c_copy(h, i):
        return remote(cout.at[h, i], cin.at[h, i], c_s.at[h, i], c_r.at[h, i], across)

    def t_copy(h, i, who):
        at = total.at[h, who, i]
        return remote(at, at, t_s.at[h, i], t_r.at[h, i], sibling)

    @loop(chunks)
    def _(i):
        sib_copy(i).start()

    @loop(chunks)
    def _(i):
        sib_copy(i).wait_recv()
        part = own[i] + fromsib[i].astype(F32)
        own[i] = part
        for h in range(2):
            cout[h, i] = part[:, h * HALF : (h + 1) * HALF].astype(BF16)
        c_copy(0, i).start()

    @loop(chunks)
    def _(i):
        c_copy(1, i).start()

    turned = basis_ref[rows_of(y, 256), :].astype(F32).T
    for h in range(2):
        for w in range(NXH):
            bt[h, w * NZ : (w + 1) * NZ] = turned[
                h * HALF : (h + 1) * HALF, w * 128 : (w + 1) * 128
            ].reshape(NZ, 16, 128)
    acc[...] = jnp.zeros_like(acc)

    def add_terms(h, tot, k):
        for j in range(NY):
            acc[h, j] += lax.dot_general(
                tot, acts[rows_of(k, CHUNK), j * 256 : (j + 1) * 256], ROW_CONTRACT, preferred_element_type=F32
            )

    def take(h, i):
        c_copy(h, i).wait_recv()
        tot = (own[i, :, h * HALF : (h + 1) * HALF] + cin[h, i].astype(F32)).astype(BF16)
        total[h, core, i] = tot
        t_copy(h, i, core).start()
        add_terms(h, tot, mine + i)
        t_copy(h, i, 1 - core).wait_recv()
        add_terms(h, total[h, 1 - core, i], their + i)

    def y_copy(h, d):
        q, dev = ypeer(d)
        return remote(ysend.at[h, q], yrecv.at[h, d], y_s.at[h, d], y_r.at[h, d], dev)

    def z_copy(h, d):
        q, dev = zxpeer(d)
        return remote(zsend.at[h, q], zrecv.at[h, d], z_s.at[h, d], z_r.at[h, d], dev)

    def az_copy(h, part, d):
        at = ct.at[part, h, y, zx]
        return remote(at, at, az_s.at[part, h, d], az_r.at[part, h, d], zxpeer(d)[1])

    def ay_copy(h, part, d):
        at = ct.at[part, h, y]
        return remote(at, at, ay_s.at[part, h, d], ay_r.at[part, h, d], ypeer(d)[1])

    def scatter_y(h):
        ysend[h] = acc[h].astype(BF16)

        @loop(NY, 1)
        def _(d):
            y_copy(h, d).start()

    def scatter_zx(h):
        s = acc[h, y]
        for d in range(1, NY):
            y_copy(h, d).wait_recv()
            s = s + yrecv[h, d].astype(F32)
        for w in range(NXH):
            s32[h, w * NZ : (w + 1) * NZ] = s[:, w * 128 : (w + 1) * 128].reshape(NZ, 16, 128)
        zsend[h] = s32[h].astype(BF16)

        @loop(nzx, 1)
        def _(d):
            z_copy(h, d).start()

    def gather_zx(h):
        def add_z(d, s):
            z_copy(h, d).wait_recv()
            return s + zrecv[h, d].astype(F32)

        block = lax.fori_loop(1, nzx, add_z, s32[h, zx]) / F32(rows_total) + bt[h, zx]
        upper = block.astype(BF16)
        ct[0, h, y, zx] = upper
        ct[1, h, y, zx] = (block - upper.astype(F32)).astype(BF16)
        for part in range(2):

            @loop(nzx, 1)
            def _(d, part=part):
                az_copy(h, part, d).start()

    def gather_y(h, part):
        @loop(nzx, 1)
        def _(d):
            az_copy(h, part, d).wait_recv()

        @loop(NY, 1)
        def _(d):
            ay_copy(h, part, d).start()

    def gathered(h, part):
        @loop(NY, 1)
        def _(d):
            ay_copy(h, part, d).wait_recv()

    loop(chunks)(lambda i: take(0, i))
    scatter_y(0)
    loop(chunks // 2 + 1)(lambda i: take(1, i))
    scatter_zx(0)
    loop(chunks, chunks // 2 + 1)(lambda i: take(1, i))
    scatter_y(1)
    gather_zx(0)
    scatter_zx(1)
    gather_y(0, 0)
    gather_y(0, 1)
    gather_zx(1)
    gather_y(1, 0)
    gather_y(1, 1)
    gathered(0, 0)
    gathered(1, 0)

    def piece(part, j):
        rows = []
        for h in range(2):
            both = ct[part, h, j]
            rows.append(
                jnp.concatenate([both[w * NZ : (w + 1) * NZ].reshape(HALF, 128) for w in range(NXH)], axis=1)
            )
        return jnp.concatenate(rows, axis=0)

    gram = jnp.zeros((256, 256), F32)
    for j in range(NY):
        high = piece(0, j)
        gram += lax.dot_general(high, high, LANE_CONTRACT, preferred_element_type=F32)
    g[...] = gram.reshape(g.shape)
    first = remote(g, gsib, g_s.at[0], g_r.at[0], sibling)
    first.start()
    first.wait_recv()
    gx[...] = g[...] + gsib[...]
    second = remote(gx.at[core], gc, g_s.at[1], g_r.at[1], across)
    second.start()
    gathered(0, 1)
    gathered(1, 1)
    weighted = jnp.zeros((256, 128), F32)
    for j in range(NY):
        full = piece(0, j).astype(F32) + piece(1, j).astype(F32)
        for w in range(2):
            at = j * 256 + w * 128
            weighted += full[:, w * 128 : (w + 1) * 128] * center_ref[:, at : at + 128]
    seen = jnp.sum(weighted, axis=1, keepdims=True)
    second.wait_recv()
    gtot[core] = gx[core] + gc[...]
    third = remote(gtot.at[core], gtot.at[core], g_s.at[2], g_r.at[2], sibling)
    third.start()
    third.wait_recv()

    inverse = factor_inverse(gtot[...].reshape(256, 256))
    w_hi = inverse.astype(BF16)
    w_lo = (inverse - w_hi.astype(F32)).astype(BF16)
    dims = (((0,), (1,)), ((), ()))
    for j in range(NY):
        high, low = piece(0, j), piece(1, j)
        q = lax.dot_general(high, w_lo, dims, preferred_element_type=F32)
        q += lax.dot_general(low, w_hi, dims, preferred_element_type=F32)
        q += lax.dot_general(high, w_hi, dims, preferred_element_type=F32)
        ortho_ref[j * 256 : (j + 1) * 256, :] = q
        qb[j * 256 : (j + 1) * 256, :] = q.astype(BF16)
    offset = jnp.sum(inverse.T * seen, axis=0, keepdims=True)

    def first_chunk(there, c):
        return ((xl + there - 2 * xl * there) * 2 + c) * qchunks

    def part_of(k):
        return jnp.dot(acts[rows_of(k, CHUNK), :], qb[...], preferred_element_type=F32) - offset

    def p_copy(slot, i):
        return remote(ptosib.at[slot, i], pfromsib.at[slot, i], p_s.at[slot, i], p_r.at[slot, i], sibling)

    def pc_copy(i):
        return remote(pout.at[i], pin.at[i], pc_s.at[i], pc_r.at[i], across)

    def give(slot, i):
        ptosib[slot, i] = part_of(first_chunk(1 - slot, 1 - core) + i)
        p_copy(slot, i).start()

    loop(qchunks)(lambda i: give(0, i))

    @loop(qchunks)
    def _(i):
        part = part_of(first_chunk(1, core) + i)
        p_copy(0, i).wait_recv()
        pout[i] = (part + pfromsib[0, i]).astype(BF16)
        pc_copy(i).start()

    loop(qchunks)(lambda i: give(1, i))

    @loop(qchunks)
    def _(i):
        part = part_of(first_chunk(0, core) + i)
        p_copy(1, i).wait_recv()
        mine32[i] = part + pfromsib[1, i]

    second_moment = jnp.zeros((256, 256), F32)
    first_moment = jnp.zeros((256, 128), F32)
    ones = jnp.ones((CHUNK, 128), BF16)
    base = pl.multiple_of((xl * 2 + core) * quarter, quarter)
    count = jnp.sum(mask_ref[:, pl.ds(base, quarter)].astype(F32), keepdims=True)
    for i in range(qchunks):
        pc_copy(i).wait_recv()
        score = (mine32[i] + pin[i].astype(F32)).astype(BF16)
        scores_ref[i * CHUNK : (i + 1) * CHUNK, :] = score
        weight = mask_ref[:, pl.ds(pl.multiple_of(base + i * CHUNK, CHUNK), CHUNK)].astype(F32)
        chosen = (score.astype(F32).T * weight).astype(BF16)
        second_moment += jnp.dot(chosen, score, preferred_element_type=F32)
        first_moment += jnp.dot(chosen, ones, preferred_element_type=F32)
    lane = lax.broadcasted_iota(jnp.int32, first_moment.shape, 1)
    mom[:, :, :, 0:256] = second_moment.reshape(2, nxy, 8, 256)
    mom[:, :, :, 256:384] = jnp.where(lane == 1, count, first_moment).reshape(2, nxy, 8, 128)

    halves = remote(mom.at[1 - core], mrecv, m_s.at[0], m_r.at[0], sibling)
    halves.start()
    halves.wait_recv()
    hsum[...] = mom[core] + mrecv[...]

    def x_copy(d):
        q, dev = xypeer(d)
        return remote(hsum.at[q], xrecv.at[d], x_s.at[d], x_r.at[d], dev)

    @loop(nxy, 1)
    def _(d):
        x_copy(d).start()

    def add_x(d, s):
        x_copy(d).wait_recv()
        return s + xrecv[d]

    zbuf[z] = lax.fori_loop(1, nxy, add_x, hsum[xy])

    def zz_copy(d):
        return remote(zbuf.at[z], zbuf.at[z], zz_s.at[d], zz_r.at[d], zpeer(d))

    @loop(NZ, 1)
    def _(d):
        zz_copy(d).start()

    @loop(NZ, 1)
    def _(d):
        zz_copy(d).wait_recv()

    tot = zbuf[0]
    for d in range(1, NZ):
        tot = tot + zbuf[d]
    fin[core, xy] = tot

    def ax_copy(d):
        return remote(fin.at[core, xy], fin.at[core, xy], ax_s.at[d], ax_r.at[d], xypeer(d)[1])

    @loop(nxy, 1)
    def _(d):
        ax_copy(d).start()

    @loop(nxy, 1)
    def _(d):
        ax_copy(d).wait_recv()

    whole = remote(fin.at[core], fin.at[core], m_s.at[1], m_r.at[1], sibling)
    whole.start()
    whole.wait_recv()
    moments_ref[...] = fin[...].reshape(moments_ref.shape)

    @loop(chunks)
    def _(i):
        sib_copy(i).wait_send()
        for h in range(2):
            c_copy(h, i).wait_send()
            t_copy(h, i, core).wait_send()

    @loop(NY, 1)
    def _(d):
        for h in range(2):
            y_copy(h, d).wait_send()
            for part in range(2):
                ay_copy(h, part, d).wait_send()

    @loop(nzx, 1)
    def _(d):
        for h in range(2):
            z_copy(h, d).wait_send()
            for part in range(2):
                az_copy(h, part, d).wait_send()

    @loop(qchunks)
    def _(i):
        for slot in range(2):
            p_copy(slot, i).wait_send()
        pc_copy(i).wait_send()

    @loop(nxy, 1)
    def _(d):
        x_copy(d).wait_send()
        ax_copy(d).wait_send()

    @loop(NZ, 1)
    def _(d):
        zz_copy(d).wait_send()

    for copy in (first, second, third, halves, whole):
        copy.wait_send()


def step_call(acts, basis, center, mask, rows_total):
    rows, cols = acts.shape
    k = basis.shape[1]
    chunks = rows // CHUNK // 2
    qchunks = rows // CHUNK // 4
    nzx = NZ * NXH
    nxy = 4 * NY
    wide = k + 128
    dma = pltpu.SemaphoreType.DMA
    vm = pltpu.VMEM
    half = (2, k // 2, k)
    return pl.pallas_call(
        functools.partial(step_kernel, rows_total),
        out_shape=(
            jax.ShapeDtypeStruct((cols, k), F32),
            jax.ShapeDtypeStruct((rows // 4, k), BF16),
            jax.ShapeDtypeStruct((k, wide), F32),
        ),
        in_specs=[pl.BlockSpec(memory_space=pl.ANY)] + [pl.BlockSpec(memory_space=vm)] * 3,
        out_specs=(pl.BlockSpec(memory_space=vm),) * 3,
        scratch_shapes=[
            vm((rows, cols), BF16),
            vm((chunks, CHUNK, k), BF16),
            vm((chunks, CHUNK, k), BF16),
            vm((chunks, CHUNK, k), F32),
            vm((2, chunks, CHUNK, HALF), BF16),
            vm((2, chunks, CHUNK, HALF), BF16),
            vm((2, 2, chunks, CHUNK, HALF), BF16),
            vm((2, NY, HALF, 256), F32),
            vm((2, NY, HALF, 256), BF16),
            vm((2, NY, HALF, 256), BF16),
            vm((2, nzx, 16, 128), F32),
            vm((2, nzx, 16, 128), BF16),
            vm((2, nzx, 16, 128), BF16),
            vm((2, nzx, 16, 128), F32),
            vm((2, 2, NY, nzx, 16, 128), BF16),
            vm(half, F32),
            vm(half, F32),
            vm(half, F32),
            vm((k // 2, k), F32),
            vm(half, F32),
            vm((cols, k), BF16),
            vm((2, qchunks, CHUNK, k), F32),
            vm((2, qchunks, CHUNK, k), F32),
            vm((qchunks, CHUNK, k), BF16),
            vm((qchunks, CHUNK, k), BF16),
            vm((qchunks, CHUNK, k), F32),
            vm((2, nxy, 8, wide), F32),
            vm((nxy, 8, wide), F32),
            vm((nxy, 8, wide), F32),
            vm((nxy, 8, wide), F32),
            vm((NZ, 8, wide), F32),
            vm((2, nxy, 8, wide), F32),
            dma((2 * chunks,)),
            dma((chunks,)),
            dma((chunks,)),
        ]
        + [dma((2, chunks))] * 4
        + [dma((2, NY))] * 2
        + [dma((2, nzx))] * 2
        + [dma((2, 2, nzx))] * 2
        + [dma((2, 2, NY))] * 2
        + [dma((3,))] * 2
        + [dma((2, qchunks))] * 2
        + [dma((qchunks,))] * 2
        + [dma((2,))] * 2
        + [dma((nxy,))] * 2
        + [dma((NZ,))] * 2
        + [dma((nxy,))] * 2,
        compiler_params=pltpu.CompilerParams(
            collective_id=0, has_side_effects=True, vmem_limit_bytes=48 * 1024 * 1024
        ),
        name="pca_step",
    )(acts, basis, center, mask)


def finish_kernel(ortho_in, scores_in, moments_ref, ortho_ref, scores_ref, mean_ref, cov_ref):
    ortho_ref[...] = ortho_in[...]
    scores_ref[...] = scores_in[...]
    k = cov_ref.shape[0]
    second = moments_ref[:, 0:k]
    side = moments_ref[:, k : k + 128]
    weight_sum = side[0:1, 1:2]
    mean = side / jnp.maximum(weight_sum, 1.0)
    mean_row = mean.T[0:1, :]
    mean_ref[...] = mean_row
    cov_ref[...] = (second - weight_sum * (mean[:, 0:1] * mean_row)) / jnp.maximum(weight_sum - 1.0, 1.0)


def finish_call(ortho, scores, moments):
    k = ortho.shape[1]
    return pl.pallas_call(
        finish_kernel,
        out_shape=(
            jax.ShapeDtypeStruct(ortho.shape, F32),
            jax.ShapeDtypeStruct(scores.shape, BF16),
            jax.ShapeDtypeStruct((1, k), F32),
            jax.ShapeDtypeStruct((k, k), F32),
        ),
        in_specs=[pl.BlockSpec(memory_space=pltpu.VMEM)] * 3,
        out_specs=(pl.BlockSpec(memory_space=pltpu.VMEM),) * 4,
        compiler_params=pltpu.CompilerParams(vmem_limit_bytes=16 * 1024 * 1024),
        name="finish",
    )(ortho, scores, moments)


def per_device(acts, basis, center, mask):
    rows_total = acts.shape[0] * lax.axis_size("rows")
    moved = step_call(acts, basis, center[None, :], mask[None, :], rows_total)
    orthonormal, scores, mean, cov = finish_call(*moved)
    return (orthonormal, scores, mean.reshape(-1), cov)


def solution(mesh):
    placed = (P("rows", "panel"), P("panel", None), P("panel"), P("rows"))
    return jax.shard_map(
        per_device,
        mesh=mesh,
        in_specs=placed,
        out_specs=(P("panel", None), P(("rows", "panel"), None), P(), P()),
        check_vma=False,
    )
```

time: 1660 us -> 125 us (0.08); the launches traced: 1630 us -> 125 us
  waiting for transfers between devices: 1200 us -> 0 us
  blocking collectives: 313 us -> 0 us
  Pallas kernels: 0 us -> 122 us
  other arithmetic: 60.1 us -> 0 us
  matrix products: 29.2 us -> 0 us
    psum x3 -> x0, waiting for transfers between devices: 1200 us -> none  [the longest x1 659 us: per_device(): lax.psum(cross_term, 'rows') / jnp.float32(rows_total)]
    psum x3 -> x0, blocking collectives: 313 us -> none  [the longest x1 158 us: per_device(): totals = lax.psum(moments_of(score_half, mask), 'rows')]
    pallas_call x0 -> x2, Pallas kernels: none -> 122 us  [the longest x1 120 us: step_call(): pl.pallas_call(functools.partial(step_kernel, rows_total), out_shape=(jax...]
    another operation x10 -> x0, other arithmetic: 54.7 us -> none  [the longest x6 34 us: per_device(): factor = jnp.linalg.cholesky(gram_matrix)]
    dot_general x7 -> x0, matrix products: 26.9 us -> none  [the longest x1 7.71 us: per_device(): jnp.dot(acts, ortho_half, preferred_element_type=jnp.float32)]
  transfers between devices with their start and end apart: 3 -> 0, of which waited for: 3 -> 0; matrix products, arithmetic and copies ran while one was open for 0% -> 0% of each run, Pallas kernels for 0% -> 0%
where the time goes in v2:
time: 125 us
  Pallas kernels  122 us (98%)
  local copies, waits for them, and re-layouts  2.44 us (2%)
    pallas_call x1, Pallas kernels, step_call(): pl.pallas_call(functools.partial(step_kernel, rows_total), out_shape=(jax...  120 us

profile of v2, /device:TPU:1, one launch (start us, length us, event | category | flops | bytes accessed | tf_op | source)
XLA Modules:
  0.0 124.9 jit_solution(5533238482769432615)
XLA Ops:
  0.6 0.0 copy-start
  0.6 1.0 copy-done
  1.7 0.0 copy-start.1
  1.7 0.7 copy-done.1
  2.4 0.0 copy-start.2
  2.4 0.7 copy-done.2
  3.1 120.3 %pca_step.1 = (f32[1024,256]{1,0:T(8,128)S(1)}, bf16[1024,256]{1,0:T(8,128)(2,1)S(1)}, f32[256,384]{1,0:T(8,128)S(1)}) custom-call(bf16[4096,1024]{1,0:T(8,128)(2,1)} %acts_hbm.1, bf16[1024,256]{1,0:T(8,128)(2,1)S(1)} %copy-done, f32[1,1024]{1,0:T(1,128)S(1)} %bitcast.4, s32[1,4096]{1,0:T(1,128)S(1)} %bitcast.3), custom_call_target="tpu_custom_call" | custom-call | tf_op jit(solution)/shard_map/pca_step/pallas_call | solution.py:513
  123.4 1.5 %finish.1 = (f32[1024,256]{1,0:T(8,128)}, bf16[1024,256]{1,0:T(8,128)(2,1)}, f32[1,256]{1,0:T(1,128)}, f32[256,256]{1,0:T(8,128)}) custom-call(f32[1024,256]{1,0:T(8,128)S(1)} %get-tuple-element.11.ortho_in, bf16[1024,256]{1,0:T(8,128)(2,1)S(1)} %get-tuple-element.12.scores_in, f32[256,384]{1,0:T(8,128)S(1)} %get-tuple-element.13.moments_ref), custom_call_target="tpu_custom_call" | custom-call | tf_op jit(solution)/shard_map/finish/pallas_call | solution.py:593
Async XLA Ops:
  0.6 1.0 copy-start
  1.7 0.7 copy-start.1
  2.4 0.7 copy-start.2
